TPU v7x, 32 devices: a whole 2x2x4 slice. The times are simulated.
32 devices in a mesh: wide: 8 (over y, x, core), narrow: 4 (over z).
Axes of the slice: x: 2, y: 2, z: 4, core: 2. Of those that a mesh axis runs over, the one named last changes fastest.
Arguments:
- query_act: bfloat16 [64, 16384], P(None, 'wide'), may hold values from -6 to 6
- query_grad: bfloat16 [64, 16384], P(None, 'narrow'), may hold values from -6 to 6
- act_basis: bfloat16 [16384, 16384], P('wide', 'narrow'), may hold values from -0.046875 to 0.046875
- grad_basis: bfloat16 [16384, 16384], P('narrow', 'wide'), may hold values from -0.046875 to 0.046875
- eigenvalues: float32 [16384, 16384], P('wide', 'narrow'), may hold values from 0.1 to 10
- train_act: bfloat16 [64, 16384], P(None, 'narrow'), may hold values from -6 to 6
- train_grad: bfloat16 [64, 16384], P(None, 'wide'), may hold values from -6 to 6
Outputs:
- scores: float32 [64, 64], replicated
All inputs are finite; a program needn't handle non-finite values.
Results may differ from a plain program's by a relative error of at most 0.0057.
Values may be sent and summed in bfloat16 or wider, within the bound.
No kernel may reach another device: no remote copies, remote signals or barrier semaphores. Data moves between devices by JAX's collectives and lax.ppermute only.
A program may use at most 128 MiB of HBM per device.

v0:
```python
import jax
import jax.numpy as jnp
from jax import lax
from jax.experimental import pallas as pl
from jax.experimental.pallas import tpu as pltpu
from jax.sharding import PartitionSpec as P


BF16 = jnp.bfloat16
F32 = jnp.float32


def tile_of(extent, largest):
    return min(extent, largest)


def one_hot_rows(count, mask, dtype):
    rows = lax.broadcasted_iota(jnp.int32, (count, count), 0)
    cols = lax.broadcasted_iota(jnp.int32, (count, count), 1)
    return (cols == (rows ^ mask)).astype(F32).astype(dtype)


def rotate(mask, query, basis, pieces):
    count, inner = query.shape
    outer = basis.shape[1]
    step = tile_of(outer, max((1 << 20) // inner, 128))
    steps = outer // step
    piece = count // pieces

    def kernel(mask_ref, query_hbm, basis_hbm, *refs):
        outs = refs[:pieces]
        query_ref, mixed_ref, basis_ref, query_sem, basis_sems = refs[pieces:]
        query_copy = pltpu.make_async_copy(query_hbm, query_ref, query_sem)
        query_copy.start()
        copies = [
            pltpu.make_async_copy(
                basis_hbm.at[:, pl.ds(k * step, step)], basis_ref.at[k], basis_sems.at[k]
            )
            for k in range(steps)
        ]
        for copy in copies:
            copy.start()
        query_copy.wait()
        mixed_ref[...] = jnp.dot(
            one_hot_rows(count, mask_ref[0], BF16), query_ref[...], preferred_element_type=F32
        ).astype(BF16)
        for k in range(steps):
            copies[k].wait()
            value = jnp.dot(mixed_ref[...], basis_ref[k], preferred_element_type=F32)
            for p in range(pieces):
                part = value[p * piece:(p + 1) * piece, :]
                outs[p][:, k * step:(k + 1) * step] = part.astype(outs[p].dtype)

    hbm = pl.BlockSpec(memory_space=pltpu.HBM)
    return pl.pallas_call(
        kernel,
        out_shape=[
            jax.ShapeDtypeStruct((piece, outer), BF16 if p else F32) for p in range(pieces)
        ],
        in_specs=[pl.BlockSpec(memory_space=pltpu.SMEM), hbm, hbm],
        out_specs=[pl.BlockSpec(memory_space=pltpu.VMEM) for _ in range(pieces)],
        scratch_shapes=[
            pltpu.VMEM((count, inner), BF16),
            pltpu.VMEM((count, inner), BF16),
            pltpu.VMEM((steps, inner, step), BF16),
            pltpu.SemaphoreType.DMA,
            pltpu.SemaphoreType.DMA((steps,)),
        ],
        compiler_params=pltpu.CompilerParams(vmem_limit_bytes=40 << 20),
        cost_estimate=pl.CostEstimate(
            flops=2 * count * inner * outer, transcendentals=0, bytes_accessed=2 * inner * outer
        ),
    )(mask, query, basis)


def contract(marks, act_own, act_other, grads, train_act, train_grad, eigenvalues):
    pieces = len(grads)
    rows_piece, inner = grads[0].shape
    count = rows_piece * pieces
    half = count // 2
    trains, outer = train_act.shape
    wide_tile = tile_of(outer, 512)
    tiles = outer // wide_tile
    chunk = min(16, count)
    chunks = count // chunk
    rows = chunk * trains

    def kernel(marks_ref, own_ref, other_ref, *refs):
        grad_refs = refs[:pieces]
        ta_ref, tg_ref, eig_ref, out_ref, f_ref, rg_ref, inv_ref, acc_ref = refs[pieces:]
        step = pl.program_id(0)
        core = marks_ref[0]

        def fill(m):
            tg = tg_ref[...]
            for r in range(chunk):
                g = rg_ref[pl.ds(m * chunk + r, 1), :]
                f_ref[m, pl.ds(r * trains, trains), :] = g * tg

        def work(filling):
            inv_ref[...] = (1.0 / eig_ref[...]).astype(BF16)
            ta = ta_ref[...].astype(F32)
            if filling:
                fill(0)
            for m in range(chunks):
                w = jnp.dot(f_ref[m], inv_ref[...], preferred_element_type=F32)
                if filling and m + 1 < chunks:
                    fill(m + 1)
                at = m * chunk
                first = at < half
                a_own = own_ref[pl.ds(at % half, chunk), :]
                a_other = other_ref[pl.ds(at % half, chunk), :]
                ra = jnp.where((core == 0) == first, a_own, a_other).astype(F32)
                p = (ra[:, None, :] * ta[None, :, :]).reshape(rows, wide_tile)
                w = w * p
                lanes = w[:, :128]
                for k in range(1, wide_tile // 128):
                    lanes = lanes + w[:, k * 128:(k + 1) * 128]
                if filling:
                    acc_ref[m] = lanes
                else:
                    acc_ref[m] += lanes

        @pl.when(step == 0)
        def _():
            for k in range(pieces):
                rg_ref[pl.ds(k * rows_piece, rows_piece), :] = grad_refs[k][...]
            work(True)

        @pl.when(step > 0)
        def _():
            work(False)

        @pl.when(step == tiles - 1)
        def _():
            total = jnp.sum(acc_ref[...].reshape(count, trains, 128), axis=-1)
            out_ref[...] = jnp.dot(
                one_hot_rows(count, marks_ref[1], F32), total,
                precision=lax.Precision.HIGHEST, preferred_element_type=F32,
            )

    whole = lambda shape: pl.BlockSpec(shape, lambda n, s: tuple(0 for _ in shape))
    return pl.pallas_call(
        kernel,
        out_shape=jax.ShapeDtypeStruct((count, trains), F32),
        grid_spec=pltpu.PrefetchScalarGridSpec(
            num_scalar_prefetch=1,
            grid=(tiles,),
            in_specs=[
                pl.BlockSpec((half, wide_tile), lambda n, s: (0, n)),
                pl.BlockSpec((half, wide_tile), lambda n, s: (0, n)),
                *[whole((rows_piece, inner)) for _ in range(pieces)],
                pl.BlockSpec((trains, wide_tile), lambda n, s: (0, n)),
                whole((trains, inner)),
                pl.BlockSpec((inner, wide_tile), lambda n, s: (0, n)),
            ],
            out_specs=whole((count, trains)),
            scratch_shapes=[
                pltpu.VMEM((chunks, rows, inner), BF16),
                pltpu.VMEM((count, inner), BF16),
                pltpu.VMEM((inner, wide_tile), BF16),
                pltpu.VMEM((chunks, rows, 128), F32),
            ],
        ),
        compiler_params=pltpu.CompilerParams(vmem_limit_bytes=44 << 20),
    )(marks, act_own, act_other, *grads, train_act, train_grad, eigenvalues)


def solution(mesh):
    wide, narrow = mesh.shape["wide"], mesh.shape["narrow"]

    def swap(value, axis, size, bit):
        return lax.ppermute(value, axis, [(i, i ^ bit) for i in range(size)])

    def bits(size, start=1):
        bit = start
        while bit < size:
            yield bit
            bit *= 2

    def whole_step(query_act, query_grad, act_basis, grad_basis, eigenvalues, train_act, train_grad):
        count = query_act.shape[0]
        half, piece = count // 2, count // narrow
        core = lax.axis_index("wide") & 1
        row_mask = lax.axis_index("narrow") * piece
        act_mask = (row_mask ^ (core * half)).astype(jnp.int32).reshape(1)
        grad_mask = row_mask.astype(jnp.int32).reshape(1)
        marks = jnp.stack([core, row_mask]).astype(jnp.int32)

        grad, *leaving = rotate(grad_mask, query_grad, grad_basis, narrow)
        got = [swap(leaving[k - 1], "narrow", narrow, k) for k in range(1, narrow)]
        act, leaving = rotate(act_mask, query_act, act_basis, 2)
        paired = swap(leaving, "wide", wide, 1)
        for value in got:
            grad = grad + value.astype(F32)
        grad = grad.astype(BF16)
        grads = [grad] + [swap(grad, "narrow", narrow, k) for k in range(1, narrow)]
        act = act + paired.astype(F32)
        middle = act.shape[1] // 2
        left, right = act[:, :middle], act[:, middle:]
        order = list(bits(wide, 2))
        for bit_left, bit_right in zip(order, reversed(order)):
            from_left = swap(left.astype(BF16), "wide", wide, bit_left)
            from_right = swap(right.astype(BF16), "wide", wide, bit_right)
            left = left + from_left.astype(F32)
            right = right + from_right.astype(F32)
        own = jnp.concatenate([left.astype(BF16), right.astype(BF16)], axis=1)
        other = swap(own, "wide", wide, 1)
        scores = contract(marks, own, other, grads, train_act, train_grad, eigenvalues)
        for bit in bits(wide):
            scores = scores + swap(scores, "wide", wide, bit)
        for bit in bits(narrow):
            scores = scores + swap(scores, "narrow", narrow, bit)
        inner, outer = eigenvalues.shape
        return scores * float(inner * wide * outer * narrow) ** (-0.5)

    in_specs = (
        P(None, "wide"),
        P(None, "narrow"),
        P("wide", "narrow"),
        P("narrow", "wide"),
        P("wide", "narrow"),
        P(None, "narrow"),
        P(None, "wide"),
    )
    return jax.shard_map(whole_step, mesh=mesh, in_specs=in_specs, out_specs=P(), check_vma=False)
```

profile of v0, /device:TPU:0, one launch (start us, length us, event | category | flops | bytes accessed | tf_op | source)
XLA Modules:
  0.0 138.3 jit_solution(10050130079312929540)
XLA Ops:
  0.0 0.0 copy-start.1
  0.0 0.0 copy-start.2
  0.0 1.0 copy-done.2
  1.0 0.0 copy-start
  1.0 0.0 copy-start.3
  1.0 6.6 %shard_map.73 = (f32[32,4096]{1,0:T(8,128)S(1)}, bf16[32,4096]{1,0:T(8,128)(2,1)S(1)}) custom-call(s32[1]{0:T(128)} %bitcast.2.mask_ref, bf16[64,2048]{1,0:T(8,128)(2,1)S(1)} %copy-done.2, bf16[2048,4096]{1,0:T(8,128)(2,1)} %basis_hbm.2), custom_call_target="tpu_custom_call" | custom-call | flops 1073741824 | bytes 16777216 | tf_op jit(solution)/shard_map/pallas_call | solution.py:55
  7.6 0.6 collective-permute-start
  8.2 1.2 collective-permute-done
  9.4 2.9 %collective-permute-start.1 = (bf16[32,2048]{1,0:T(8,128)(2,1)S(1)}, bf16[32,2048]{1,0:T(8,128)(2,1)S(1)}, u32[]{:S(2)}, u32[]{:S(2)}) collective-permute-start(bf16[32,2048]{1,0:T(8,128)(2,1)S(1)} %get-tuple-element.21), channel_id=1, source_target_pairs={{0,8},{4,12},{8,0},{12,4},{16,24},{20,28},{24,16},{28,20},{1,9},{5... | collective-permute-start | bytes 393224 | tf_op jit(solution)/shard_map/ppermute | solution.py:173
  12.3 1.5 %collective-permute-start.3 = (bf16[32,2048]{1,0:T(8,128)(2,1)S(1)}, bf16[32,2048]{1,0:T(8,128)(2,1)S(1)}, u32[]{:S(2)}, u32[]{:S(2)}) collective-permute-start(bf16[32,2048]{1,0:T(8,128)(2,1)S(1)} %get-tuple-element.22), channel_id=1, source_target_pairs={{0,16},{4,20},{8,24},{12,28},{16,0},{20,4},{24,8},{28,12},{1,17},{... | collective-permute-start | bytes 393224 | tf_op jit(solution)/shard_map/ppermute | solution.py:173
  13.9 2.3 %collective-permute-done.1 = bf16[32,2048]{1,0:T(8,128)(2,1)S(1)} collective-permute-done((bf16[32,2048]{1,0:T(8,128)(2,1)S(1)}, bf16[32,2048]{1,0:T(8,128)(2,1)S(1)}, u32[]{:S(2)}, u32[]{:S(2)}) %collective-permute-start.1) | collective-permute-done | bytes 131104 | tf_op jit(solution)/shard_map/ppermute | solution.py:173
  16.1 1.5 %collective-permute-done.3 = bf16[32,2048]{1,0:T(8,128)(2,1)S(1)} collective-permute-done((bf16[32,2048]{1,0:T(8,128)(2,1)S(1)}, bf16[32,2048]{1,0:T(8,128)(2,1)S(1)}, u32[]{:S(2)}, u32[]{:S(2)}) %collective-permute-start.3) | collective-permute-done | bytes 131104 | tf_op jit(solution)/shard_map/ppermute | solution.py:173
  17.7 1.6 %collective-permute-start.2 = (bf16[32,2048]{1,0:T(8,128)(2,1)S(1)}, bf16[32,2048]{1,0:T(8,128)(2,1)S(1)}, u32[]{:S(2)}, u32[]{:S(2)}) collective-permute-start(bf16[32,2048]{1,0:T(8,128)(2,1)S(1)} %get-tuple-element.19), channel_id=1, source_target_pairs={{0,16},{4,20},{8,24},{12,28},{16,0},{20,4},{24,8},{28,12},{1,17},{... | collective-permute-start | bytes 393224 | tf_op jit(solution)/shard_map/ppermute | solution.py:173
  19.2 0.5 collective-permute-start.4
  19.8 0.0 copy-done.1
  19.8 7.5 %shard_map.74 = (f32[16,2048]{1,0:T(8,128)S(1)}, bf16[16,2048]{1,0:T(8,128)(2,1)S(1)}, bf16[16,2048]{1,0:T(8,128)(2,1)S(1)}, bf16[16,2048]{1,0:T(8,128)(2,1)S(1)}) custom-call(s32[1]{0:T(128)} %bitcast.1.mask_ref, bf16[64,4096]{1,0:T(8,128)(2,1)S(1)} %copy-done.1, bf16[4096,2048]{1,0:T(8,128)(2,1)} %basis_hbm.3), custom_call_target="tpu_custom_call" | custom-call | flops 1073741824 | bytes 16777216 | tf_op jit(solution)/shard_map/pallas_call | solution.py:55
  27.3 1.6 %collective-permute-start.6 = (bf16[16,2048]{1,0:T(8,128)(2,1)S(1)}, bf16[16,2048]{1,0:T(8,128)(2,1)S(1)}, u32[]{:S(2)}, u32[]{:S(2)}) collective-permute-start(bf16[16,2048]{1,0:T(8,128)(2,1)S(1)} %get-tuple-element.14), channel_id=1, source_target_pairs={{0,1},{1,0},{2,3},{3,2},{4,5},{5,4},{6,7},{7,6},{8,9},{9,8},{10,11... | collective-permute-start | bytes 196616 | tf_op jit(solution)/shard_map/ppermute | solution.py:173
  28.9 2.6 %collective-permute-start.7 = (bf16[16,2048]{1,0:T(8,128)(2,1)S(1)}, bf16[16,2048]{1,0:T(8,128)(2,1)S(1)}, u32[]{:S(2)}, u32[]{:S(2)}) collective-permute-start(bf16[16,2048]{1,0:T(8,128)(2,1)S(1)} %get-tuple-element.15), channel_id=1, source_target_pairs={{0,2},{1,3},{2,0},{3,1},{4,6},{5,7},{6,4},{7,5},{8,10},{9,11},{10,... | collective-permute-start | bytes 196616 | tf_op jit(solution)/shard_map/ppermute | solution.py:173
  31.5 0.2 collective-permute-start.8
  31.7 0.0 collective-permute-done.2
  31.7 0.0 collective-permute-done.4
  31.7 0.1 add_convert_fusion.1
  31.8 0.1 collective-permute-start.5
  31.9 0.0 collective-permute-done.6
  31.9 3.5 %collective-permute-done.7 = bf16[16,2048]{1,0:T(8,128)(2,1)S(1)} collective-permute-done((bf16[16,2048]{1,0:T(8,128)(2,1)S(1)}, bf16[16,2048]{1,0:T(8,128)(2,1)S(1)}, u32[]{:S(2)}, u32[]{:S(2)}) %collective-permute-start.7) | collective-permute-done | bytes 65568 | tf_op jit(solution)/shard_map/ppermute | solution.py:173
  35.5 2.6 %collective-permute-done.8 = bf16[16,2048]{1,0:T(8,128)(2,1)S(1)} collective-permute-done((bf16[16,2048]{1,0:T(8,128)(2,1)S(1)}, bf16[16,2048]{1,0:T(8,128)(2,1)S(1)}, u32[]{:S(2)}, u32[]{:S(2)}) %collective-permute-start.8) | collective-permute-done | bytes 65568 | tf_op jit(solution)/shard_map/ppermute | solution.py:173
  38.2 0.1 collective-permute-start.10
  38.2 1.0 collective-permute-start.11
  39.2 2.5 %collective-permute-start.9 = (bf16[16,2048]{1,0:T(8,128)(2,1)S(1)}, bf16[16,2048]{1,0:T(8,128)(2,1)S(1)}, u32[]{:S(2)}, u32[]{:S(2)}) collective-permute-start(bf16[16,2048]{1,0:T(8,128)(2,1)S(1)} %add_convert_fusion.2.refs_0_), channel_id=1, source_target_pairs={{0,1},{1,0},{2,3},{3,2},{4,5},{5,4},{6,7},{7,6},{8,9},{9,8},{10,11... | collective-permute-start | bytes 196616 | tf_op jit(solution)/shard_map/ppermute | solution.py:173
  41.7 0.1 pad_add_fusion.marks_ref
  41.8 1.6 %collective-permute-done.10.refs_2_ = bf16[16,2048]{1,0:T(8,128)(2,1)S(1)} collective-permute-done((bf16[16,2048]{1,0:T(8,128)(2,1)S(1)}, bf16[16,2048]{1,0:T(8,128)(2,1)S(1)}, u32[]{:S(2)}, u32[]{:S(2)}) %collective-permute-start.10) | collective-permute-done | bytes 65568 | tf_op jit(solution)/shard_map/ppermute | solution.py:173
  43.4 1.1 collective-permute-done.11.refs_3_
  44.5 0.3 collective-permute-done.9.refs_1_
  44.8 0.0 collective-permute-done.5.other_ref
  44.8 0.0 copy-done
  44.8 0.0 copy-done.3
  44.8 75.0 %shard_map.75 = f32[64,64]{1,0:T(8,128)S(1)} custom-call(s32[2]{0:T(128)S(1)} %pad_add_fusion.marks_ref, bf16[32,4096]{1,0:T(8,128)(2,1)S(1)} %pad_maximum_fusion.own_ref, bf16[32,4096]{1,0:T(8,128)(2,1)S(1)} %collective-permute-done.5.other_ref, bf16[16,2048]{1,0:T(8,128)(2,1)S(1)} %add_convert_fusion.2.refs_0_, ...), custom_call_target="tpu_custom_call" | custom-call | tf_op jit(solution)/shard_map/pallas_call | solution.py:143
  119.8 0.1 collective-permute-start.12
  119.9 1.2 collective-permute-done.12
  121.1 1.5 %collective-permute-start.13 = (f32[64,64]{1,0:T(8,128)S(1)}, f32[64,64]{1,0:T(8,128)S(1)}, u32[]{:S(2)}, u32[]{:S(2)}) collective-permute-start(f32[64,64]{1,0:T(8,128)S(1)} %add.47), channel_id=1, source_target_pairs={{0,8},{4,12},{8,0},{12,4},{16,24},{20,28},{24,16},{28,20},{1,9},{5... | collective-permute-start | bytes 49160 | tf_op jit(solution)/shard_map/ppermute | solution.py:173
  122.6 2.4 %collective-permute-done.13 = f32[64,64]{1,0:T(8,128)S(1)} collective-permute-done((f32[64,64]{1,0:T(8,128)S(1)}, f32[64,64]{1,0:T(8,128)S(1)}, u32[]{:S(2)}, u32[]{:S(2)}) %collective-permute-start.13) | collective-permute-done | bytes 16416 | tf_op jit(solution)/shard_map/ppermute | solution.py:173
  125.0 0.5 collective-permute-start.14
  125.5 3.4 %collective-permute-done.14 = f32[64,64]{1,0:T(8,128)S(1)} collective-permute-done((f32[64,64]{1,0:T(8,128)S(1)}, f32[64,64]{1,0:T(8,128)S(1)}, u32[]{:S(2)}, u32[]{:S(2)}) %collective-permute-start.14) | collective-permute-done | bytes 16416 | tf_op jit(solution)/shard_map/ppermute | solution.py:173
  128.9 1.2 collective-permute-start.15
  130.1 2.7 %collective-permute-done.15 = f32[64,64]{1,0:T(8,128)S(1)} collective-permute-done((f32[64,64]{1,0:T(8,128)S(1)}, f32[64,64]{1,0:T(8,128)S(1)}, u32[]{:S(2)}, u32[]{:S(2)}) %collective-permute-start.15) | collective-permute-done | bytes 16416 | tf_op jit(solution)/shard_map/ppermute | solution.py:173
  132.9 0.8 collective-permute-start.16
  133.7 4.0 %collective-permute-done.16 = f32[64,64]{1,0:T(8,128)S(1)} collective-permute-done((f32[64,64]{1,0:T(8,128)S(1)}, f32[64,64]{1,0:T(8,128)S(1)}, u32[]{:S(2)}, u32[]{:S(2)}) %collective-permute-start.16) | collective-permute-done | bytes 16416 | tf_op jit(solution)/shard_map/ppermute | solution.py:173
  137.7 0.6 add_multiply_fusion
  (9 shorter events, 0.2 us)
Async XLA Ops:
  0.0 19.8 %copy-start.1 = (bf16[64,4096]{1,0:T(8,128)(2,1)S(1)}, bf16[64,4096]{1,0:T(8,128)(2,1)}, u32[]{:S(2)}) copy-start(bf16[64,4096]{1,0:T(8,128)(2,1)} %query_hbm.3) | copy-start | bytes 1572868
  0.0 1.0 copy-start.2
  1.0 43.8 %copy-start = (bf16[64,4096]{1,0:T(8,128)(2,1)S(1)}, bf16[64,4096]{1,0:T(8,128)(2,1)}, u32[]{:S(2)}) copy-start(bf16[64,4096]{1,0:T(8,128)(2,1)} %refs_4_.1) | copy-start | bytes 1572868
  1.0 43.8 %copy-start.3 = (bf16[64,2048]{1,0:T(8,128)(2,1)S(1)}, bf16[64,2048]{1,0:T(8,128)(2,1)}, u32[]{:S(2)}) copy-start(bf16[64,2048]{1,0:T(8,128)(2,1)} %refs_5_.1) | copy-start | bytes 786436
  7.6 1.7 %collective-permute-start = (bf16[32,4096]{1,0:T(8,128)(2,1)S(1)}, bf16[32,4096]{1,0:T(8,128)(2,1)S(1)}, u32[]{:S(2)}, u32[]{:S(2)}) collective-permute-start(bf16[32,4096]{1,0:T(8,128)(2,1)S(1)} %get-tuple-element.12), channel_id=1, source_target_pairs={{0,4},{4,0},{8,12},{12,8},{16,20},{20,16},{24,28},{28,24},{1,5},{5... | collective-permute-start | bytes 786440 | tf_op jit(solution)/shard_map/ppermute | solution.py:173
  9.4 6.7 %collective-permute-start.1 = (bf16[32,2048]{1,0:T(8,128)(2,1)S(1)}, bf16[32,2048]{1,0:T(8,128)(2,1)S(1)}, u32[]{:S(2)}, u32[]{:S(2)}) collective-permute-start(bf16[32,2048]{1,0:T(8,128)(2,1)S(1)} %get-tuple-element.21), channel_id=1, source_target_pairs={{0,8},{4,12},{8,0},{12,4},{16,24},{20,28},{24,16},{28,20},{1,9},{5... | collective-permute-start | bytes 393224 | tf_op jit(solution)/shard_map/ppermute | solution.py:173
  12.3 5.3 %collective-permute-start.3 = (bf16[32,2048]{1,0:T(8,128)(2,1)S(1)}, bf16[32,2048]{1,0:T(8,128)(2,1)S(1)}, u32[]{:S(2)}, u32[]{:S(2)}) collective-permute-start(bf16[32,2048]{1,0:T(8,128)(2,1)S(1)} %get-tuple-element.22), channel_id=1, source_target_pairs={{0,16},{4,20},{8,24},{12,28},{16,0},{20,4},{24,8},{28,12},{1,17},{... | collective-permute-start | bytes 393224 | tf_op jit(solution)/shard_map/ppermute | solution.py:173
  17.7 14.1 %collective-permute-start.2 = (bf16[32,2048]{1,0:T(8,128)(2,1)S(1)}, bf16[32,2048]{1,0:T(8,128)(2,1)S(1)}, u32[]{:S(2)}, u32[]{:S(2)}) collective-permute-start(bf16[32,2048]{1,0:T(8,128)(2,1)S(1)} %get-tuple-element.19), channel_id=1, source_target_pairs={{0,16},{4,20},{8,24},{12,28},{16,0},{20,4},{24,8},{28,12},{1,17},{... | collective-permute-start | bytes 393224 | tf_op jit(solution)/shard_map/ppermute | solution.py:173
  19.2 12.5 %collective-permute-start.4 = (bf16[32,2048]{1,0:T(8,128)(2,1)S(1)}, bf16[32,2048]{1,0:T(8,128)(2,1)S(1)}, u32[]{:S(2)}, u32[]{:S(2)}) collective-permute-start(bf16[32,2048]{1,0:T(8,128)(2,1)S(1)} %get-tuple-element.20), channel_id=1, source_target_pairs={{0,8},{4,12},{8,0},{12,4},{16,24},{20,28},{24,16},{28,20},{1,9},{5... | collective-permute-start | bytes 393224 | tf_op jit(solution)/shard_map/ppermute | solution.py:173
  27.3 4.7 %collective-permute-start.6 = (bf16[16,2048]{1,0:T(8,128)(2,1)S(1)}, bf16[16,2048]{1,0:T(8,128)(2,1)S(1)}, u32[]{:S(2)}, u32[]{:S(2)}) collective-permute-start(bf16[16,2048]{1,0:T(8,128)(2,1)S(1)} %get-tuple-element.14), channel_id=1, source_target_pairs={{0,1},{1,0},{2,3},{3,2},{4,5},{5,4},{6,7},{7,6},{8,9},{9,8},{10,11... | collective-permute-start | bytes 196616 | tf_op jit(solution)/shard_map/ppermute | solution.py:173
  28.9 6.6 %collective-permute-start.7 = (bf16[16,2048]{1,0:T(8,128)(2,1)S(1)}, bf16[16,2048]{1,0:T(8,128)(2,1)S(1)}, u32[]{:S(2)}, u32[]{:S(2)}) collective-permute-start(bf16[16,2048]{1,0:T(8,128)(2,1)S(1)} %get-tuple-element.15), channel_id=1, source_target_pairs={{0,2},{1,3},{2,0},{3,1},{4,6},{5,7},{6,4},{7,5},{8,10},{9,11},{10,... | collective-permute-start | bytes 196616 | tf_op jit(solution)/shard_map/ppermute | solution.py:173
  31.5 6.6 %collective-permute-start.8 = (bf16[16,2048]{1,0:T(8,128)(2,1)S(1)}, bf16[16,2048]{1,0:T(8,128)(2,1)S(1)}, u32[]{:S(2)}, u32[]{:S(2)}) collective-permute-start(bf16[16,2048]{1,0:T(8,128)(2,1)S(1)} %get-tuple-element.16), channel_id=1, source_target_pairs={{0,3},{1,2},{2,1},{3,0},{4,7},{5,6},{6,5},{7,4},{8,11},{9,10},{10,... | collective-permute-start | bytes 196616 | tf_op jit(solution)/shard_map/ppermute | solution.py:173
  31.8 13.0 %collective-permute-start.5 = (bf16[32,4096]{1,0:T(8,128)(2,1)S(1)}, bf16[32,4096]{1,0:T(8,128)(2,1)S(1)}, u32[]{:S(2)}, u32[]{:S(2)}) collective-permute-start(bf16[32,4096]{1,0:T(8,128)(2,1)S(1)} %pad_maximum_fusion.own_ref), channel_id=1, source_target_pairs={{0,4},{4,0},{8,12},{12,8},{16,20},{20,16},{24,28},{28,24},{1,5},{5... | collective-permute-start | bytes 786440 | tf_op jit(solution)/shard_map/ppermute | solution.py:173
  38.2 5.2 %collective-permute-start.10 = (bf16[16,2048]{1,0:T(8,128)(2,1)S(1)}, bf16[16,2048]{1,0:T(8,128)(2,1)S(1)}, u32[]{:S(2)}, u32[]{:S(2)}) collective-permute-start(bf16[16,2048]{1,0:T(8,128)(2,1)S(1)} %add_convert_fusion.2.refs_0_), channel_id=1, source_target_pairs={{0,2},{1,3},{2,0},{3,1},{4,6},{5,7},{6,4},{7,5},{8,10},{9,11},{10,... | collective-permute-start | bytes 196616 | tf_op jit(solution)/shard_map/ppermute | solution.py:173
  38.2 6.2 %collective-permute-start.11 = (bf16[16,2048]{1,0:T(8,128)(2,1)S(1)}, bf16[16,2048]{1,0:T(8,128)(2,1)S(1)}, u32[]{:S(2)}, u32[]{:S(2)}) collective-permute-start(bf16[16,2048]{1,0:T(8,128)(2,1)S(1)} %add_convert_fusion.2.refs_0_), channel_id=1, source_target_pairs={{0,3},{1,2},{2,1},{3,0},{4,7},{5,6},{6,5},{7,4},{8,11},{9,10},{10,... | collective-permute-start | bytes 196616 | tf_op jit(solution)/shard_map/ppermute | solution.py:173
  39.2 5.6 %collective-permute-start.9 = (bf16[16,2048]{1,0:T(8,128)(2,1)S(1)}, bf16[16,2048]{1,0:T(8,128)(2,1)S(1)}, u32[]{:S(2)}, u32[]{:S(2)}) collective-permute-start(bf16[16,2048]{1,0:T(8,128)(2,1)S(1)} %add_convert_fusion.2.refs_0_), channel_id=1, source_target_pairs={{0,1},{1,0},{2,3},{3,2},{4,5},{5,4},{6,7},{7,6},{8,9},{9,8},{10,11... | collective-permute-start | bytes 196616 | tf_op jit(solution)/shard_map/ppermute | solution.py:173
  119.8 1.3 collective-permute-start.12
  121.1 3.9 %collective-permute-start.13 = (f32[64,64]{1,0:T(8,128)S(1)}, f32[64,64]{1,0:T(8,128)S(1)}, u32[]{:S(2)}, u32[]{:S(2)}) collective-permute-start(f32[64,64]{1,0:T(8,128)S(1)} %add.47), channel_id=1, source_target_pairs={{0,8},{4,12},{8,0},{12,4},{16,24},{20,28},{24,16},{28,20},{1,9},{5... | collective-permute-start | bytes 49160 | tf_op jit(solution)/shard_map/ppermute | solution.py:173
  125.0 3.9 %collective-permute-start.14 = (f32[64,64]{1,0:T(8,128)S(1)}, f32[64,64]{1,0:T(8,128)S(1)}, u32[]{:S(2)}, u32[]{:S(2)}) collective-permute-start(f32[64,64]{1,0:T(8,128)S(1)} %add.48), channel_id=1, source_target_pairs={{0,16},{4,20},{8,24},{12,28},{16,0},{20,4},{24,8},{28,12},{1,17},{... | collective-permute-start | bytes 49160 | tf_op jit(solution)/shard_map/ppermute | solution.py:173
  128.9 3.9 %collective-permute-start.15 = (f32[64,64]{1,0:T(8,128)S(1)}, f32[64,64]{1,0:T(8,128)S(1)}, u32[]{:S(2)}, u32[]{:S(2)}) collective-permute-start(f32[64,64]{1,0:T(8,128)S(1)} %add.49), channel_id=1, source_target_pairs={{0,1},{1,0},{2,3},{3,2},{4,5},{5,4},{6,7},{7,6},{8,9},{9,8},{10,11... | collective-permute-start | bytes 49160 | tf_op jit(solution)/shard_map/ppermute | solution.py:173
  132.9 4.8 %collective-permute-start.16 = (f32[64,64]{1,0:T(8,128)S(1)}, f32[64,64]{1,0:T(8,128)S(1)}, u32[]{:S(2)}, u32[]{:S(2)}) collective-permute-start(f32[64,64]{1,0:T(8,128)S(1)} %add.50), channel_id=1, source_target_pairs={{0,2},{1,3},{2,0},{3,1},{4,6},{5,7},{6,4},{7,5},{8,10},{9,11},{10,... | collective-permute-start | bytes 49160 | tf_op jit(solution)/shard_map/ppermute | solution.py:173
where the time goes:
time: 138 us
  Pallas kernels  89.1 us (65%)
  waiting for transfers between devices  27.9 us (20%)
  starting transfers between devices  19.3 us (14%)
    pallas_call x1, Pallas kernels, contract(): pl.pallas_call(kernel, out_shape=jax.ShapeDtypeStruct((count, trains), F3...  75 us
    ppermute x17, waiting for transfers between devices, swap(): return lax.ppermute(value, axis, [(i, i ^ bit) for i in range(size)])  27.9 us
    ppermute x17, starting transfers between devices, swap(): return lax.ppermute(value, axis, [(i, i ^ bit) for i in range(size)])  19.3 us
    pallas_call x2, Pallas kernels, rotate(): pl.pallas_call(kernel, out_shape=[jax.ShapeDtypeStruct((piece, outer), BF...  14.1 us
  transfers between devices with their start and end apart: 17, of which 13 were waited for; matrix products, arithmetic and copies ran while one was open for 0% of the time, Pallas kernels for 5%

commit v1 on v0

--- a/solution.py
+++ b/solution.py
@@ -23,8 +23,9 @@
 def rotate(mask, query, basis, pieces):
     count, inner = query.shape
     outer = basis.shape[1]
-    step = tile_of(outer, max((1 << 20) // inner, 128))
-    steps = outer // step
+    deep = tile_of(inner, 2048)
+    step = tile_of(outer, max((1 << 20) // deep, 128))
+    steps, depths = outer // step, inner // deep
     piece = count // pieces
 
     def kernel(mask_ref, query_hbm, basis_hbm, *refs):
@@ -33,20 +34,31 @@
         query_copy = pltpu.make_async_copy(query_hbm, query_ref, query_sem)
         query_copy.start()
         copies = [
-            pltpu.make_async_copy(
-                basis_hbm.at[:, pl.ds(k * step, step)], basis_ref.at[k], basis_sems.at[k]
-            )
+            [
+                pltpu.make_async_copy(
+                    basis_hbm.at[pl.ds(d * deep, deep), pl.ds(k * step, step)],
+                    basis_ref.at[k, d],
+                    basis_sems.at[k, d],
+                )
+                for d in range(depths)
+            ]
             for k in range(steps)
         ]
-        for copy in copies:
-            copy.start()
+        for row in copies:
+            for copy in row:
+                copy.start()
         query_copy.wait()
         mixed_ref[...] = jnp.dot(
             one_hot_rows(count, mask_ref[0], BF16), query_ref[...], preferred_element_type=F32
         ).astype(BF16)
         for k in range(steps):
-            copies[k].wait()
-            value = jnp.dot(mixed_ref[...], basis_ref[k], preferred_element_type=F32)
+            value = jnp.zeros((count, step), F32)
+            for d in range(depths):
+                copies[k][d].wait()
+                value = value + jnp.dot(
+                    mixed_ref[:, d * deep:(d + 1) * deep], basis_ref[k, d],
+                    preferred_element_type=F32,
+                )
             for p in range(pieces):
                 part = value[p * piece:(p + 1) * piece, :]
                 outs[p][:, k * step:(k + 1) * step] = part.astype(outs[p].dtype)
@@ -62,24 +74,59 @@
         scratch_shapes=[
             pltpu.VMEM((count, inner), BF16),
             pltpu.VMEM((count, inner), BF16),
-            pltpu.VMEM((steps, inner, step), BF16),
+            pltpu.VMEM((steps, depths, deep, step), BF16),
             pltpu.SemaphoreType.DMA,
-            pltpu.SemaphoreType.DMA((steps,)),
+            pltpu.SemaphoreType.DMA((steps, depths)),
         ],
         compiler_params=pltpu.CompilerParams(vmem_limit_bytes=40 << 20),
         cost_estimate=pl.CostEstimate(
             flops=2 * count * inner * outer, transcendentals=0, bytes_accessed=2 * inner * outer
         ),
-    )(mask, query, basis)
-
-
-def contract(marks, act_own, act_other, grads, train_act, train_grad, eigenvalues):
+    )(mask, pltpu.with_memory_space_constraint(query, pltpu.HBM), basis)
+
+
+def prepare(eigenvalues):
+    inner, outer = eigenvalues.shape
+    wide_tile = tile_of(outer, 1024)
+    parts = 4
+    part = wide_tile // parts
+
+    def kernel(eig_hbm, out_ref, eig_ref, sems):
+        copies = [
+            pltpu.make_async_copy(
+                eig_hbm.at[:, pl.ds(k * part, part)], eig_ref.at[k], sems.at[k]
+            )
+            for k in range(parts)
+        ]
+        for copy in copies:
+            copy.start()
+        for k in range(parts):
+            copies[k].wait()
+            out_ref[:, k * part:(k + 1) * part] = (1.0 / eig_ref[k]).astype(BF16)
+
+    return pl.pallas_call(
+        kernel,
+        out_shape=jax.ShapeDtypeStruct((inner, wide_tile), BF16),
+        in_specs=[pl.BlockSpec(memory_space=pltpu.HBM)],
+        out_specs=pl.BlockSpec(memory_space=pltpu.VMEM),
+        scratch_shapes=[
+            pltpu.VMEM((parts, inner, part), F32),
+            pltpu.SemaphoreType.DMA((parts,)),
+        ],
+        compiler_params=pltpu.CompilerParams(vmem_limit_bytes=24 << 20),
+        cost_estimate=pl.CostEstimate(
+            flops=inner * wide_tile, transcendentals=0, bytes_accessed=6 * inner * wide_tile
+        ),
+    )(eigenvalues)
+
+
+def contract(marks, act_own, act_other, grads, train_act, train_grad, first_inverse, eigenvalues):
     pieces = len(grads)
     rows_piece, inner = grads[0].shape
     count = rows_piece * pieces
     half = count // 2
     trains, outer = train_act.shape
-    wide_tile = tile_of(outer, 512)
+    wide_tile = tile_of(outer, 1024)
     tiles = outer // wide_tile
     chunk = min(16, count)
     chunks = count // chunk
@@ -87,7 +134,8 @@
 
     def kernel(marks_ref, own_ref, other_ref, *refs):
         grad_refs = refs[:pieces]
-        ta_ref, tg_ref, eig_ref, out_ref, f_ref, rg_ref, inv_ref, acc_ref = refs[pieces:]
+        ta_ref, tg_ref, first_ref, eig_hbm, out_ref = refs[pieces:pieces + 5]
+        f_ref, rg_ref, inv_ref, acc_ref, eig_ref, eig_sems = refs[pieces + 5:]
         step = pl.program_id(0)
         core = marks_ref[0]
 
@@ -97,13 +145,22 @@
                 g = rg_ref[pl.ds(m * chunk + r, 1), :]
                 f_ref[m, pl.ds(r * trains, trains), :] = g * tg
 
+        def fetch(tile):
+            return pltpu.make_async_copy(
+                eig_hbm.at[:, pl.ds(pl.multiple_of(tile * wide_tile, wide_tile), wide_tile)],
+                eig_ref.at[tile % 2],
+                eig_sems.at[tile % 2],
+            )
+
         def work(filling):
-            inv_ref[...] = (1.0 / eig_ref[...]).astype(BF16)
+            inverse_ref = first_ref if filling else inv_ref
+            if not filling:
+                inv_ref[...] = (1.0 / eig_ref[step % 2]).astype(BF16)
             ta = ta_ref[...].astype(F32)
             if filling:
                 fill(0)
             for m in range(chunks):
-                w = jnp.dot(f_ref[m], inv_ref[...], preferred_element_type=F32)
+                w = jnp.dot(f_ref[m], inverse_ref[...], preferred_element_type=F32)
                 if filling and m + 1 < chunks:
                     fill(m + 1)
                 at = m * chunk
@@ -123,13 +180,23 @@
 
         @pl.when(step == 0)
         def _():
+            if tiles > 1:
+                fetch(1).start()
             for k in range(pieces):
                 rg_ref[pl.ds(k * rows_piece, rows_piece), :] = grad_refs[k][...]
             work(True)
 
-        @pl.when(step > 0)
-        def _():
-            work(False)
+        if tiles > 1:
+
+            @pl.when(step > 0)
+            def _():
+                fetch(step).wait()
+
+                @pl.when(step + 1 < tiles)
+                def _():
+                    fetch(step + 1).start()
+
+                work(False)
 
         @pl.when(step == tiles - 1)
         def _():
@@ -139,7 +206,9 @@
                 precision=lax.Precision.HIGHEST, preferred_element_type=F32,
             )
 
-    whole = lambda shape: pl.BlockSpec(shape, lambda n, s: tuple(0 for _ in shape))
+    whole = lambda shape: pl.BlockSpec(
+        shape, lambda n, s: tuple(0 for _ in shape), pipeline_mode=pl.Buffered(1)
+    )
     return pl.pallas_call(
         kernel,
         out_shape=jax.ShapeDtypeStruct((count, trains), F32),
@@ -152,18 +221,21 @@
                 *[whole((rows_piece, inner)) for _ in range(pieces)],
                 pl.BlockSpec((trains, wide_tile), lambda n, s: (0, n)),
                 whole((trains, inner)),
-                pl.BlockSpec((inner, wide_tile), lambda n, s: (0, n)),
+                whole((inner, wide_tile)),
+                pl.BlockSpec(memory_space=pltpu.HBM),
             ],
-            out_specs=whole((count, trains)),
+            out_specs=pl.BlockSpec((count, trains), lambda n, s: (0, 0)),
             scratch_shapes=[
                 pltpu.VMEM((chunks, rows, inner), BF16),
                 pltpu.VMEM((count, inner), BF16),
                 pltpu.VMEM((inner, wide_tile), BF16),
                 pltpu.VMEM((chunks, rows, 128), F32),
+                pltpu.VMEM((2, inner, wide_tile), F32),
+                pltpu.SemaphoreType.DMA((2,)),
             ],
         ),
-        compiler_params=pltpu.CompilerParams(vmem_limit_bytes=44 << 20),
-    )(marks, act_own, act_other, *grads, train_act, train_grad, eigenvalues)
+        compiler_params=pltpu.CompilerParams(vmem_limit_bytes=49 << 20),
+    )(marks, act_own, act_other, *grads, train_act, train_grad, first_inverse, eigenvalues)
 
 
 def solution(mesh):
@@ -199,6 +271,7 @@
         middle = act.shape[1] // 2
         left, right = act[:, :middle], act[:, middle:]
         order = list(bits(wide, 2))
+        first_inverse = prepare(eigenvalues)
         for bit_left, bit_right in zip(order, reversed(order)):
             from_left = swap(left.astype(BF16), "wide", wide, bit_left)
             from_right = swap(right.astype(BF16), "wide", wide, bit_right)
@@ -206,7 +279,9 @@
             right = right + from_right.astype(F32)
         own = jnp.concatenate([left.astype(BF16), right.astype(BF16)], axis=1)
         other = swap(own, "wide", wide, 1)
-        scores = contract(marks, own, other, grads, train_act, train_grad, eigenvalues)
+        scores = contract(
+            marks, own, other, grads, train_act, train_grad, first_inverse, eigenvalues
+        )
         for bit in bits(wide):
             scores = scores + swap(scores, "wide", wide, bit)
         for bit in bits(narrow):

time: 138 us -> 144 us (1.043)
  Pallas kernels: 89.1 us -> 97.1 us
  waiting for transfers between devices: 27.9 us -> 22.6 us
  starting transfers between devices: 19.3 us -> 21.2 us
    ppermute x17, waiting for transfers between devices: 27.9 us -> 22.6 us  [swap(): return lax.ppermute(value, axis, [(i, i ^ bit) for i in range(size)])]
    pallas_call x2, Pallas kernels: 14.1 us -> 19.1 us  [rotate(): pl.pallas_call(kernel, out_shape=[jax.ShapeDtypeStruct((piece, outer), BF...]
    pallas_call x0 -> x1, Pallas kernels: none -> 3.82 us  [prepare(): pl.pallas_call(kernel, out_shape=jax.ShapeDtypeStruct((inner, wide_tile),...]
    ppermute x17, starting transfers between devices: 19.3 us -> 21.2 us  [swap(): return lax.ppermute(value, axis, [(i, i ^ bit) for i in range(size)])]
  transfers between devices with their start and end apart: 17 -> 17, of which waited for: 13 -> 11; matrix products, arithmetic and copies ran while one was open for 0% -> 0% of each run, Pallas kernels for 5% -> 9%
where the time goes in v1:
time: 144 us
  Pallas kernels  97.1 us (67%)
  waiting for transfers between devices  22.6 us (16%)
  starting transfers between devices  21.2 us (15%)
  local copies, waits for them, and re-layouts  1.98 us (1%)
    pallas_call x1, Pallas kernels, contract(): pl.pallas_call(kernel, out_shape=jax.ShapeDtypeStruct((count, trains), F3...  74.1 us
    ppermute x17, waiting for transfers between devices, swap(): return lax.ppermute(value, axis, [(i, i ^ bit) for i in range(size)])  22.6 us
    ppermute x17, starting transfers between devices, swap(): return lax.ppermute(value, axis, [(i, i ^ bit) for i in range(size)])  21.2 us
    pallas_call x2, Pallas kernels, rotate(): pl.pallas_call(kernel, out_shape=[jax.ShapeDtypeStruct((piece, outer), BF...  19.1 us
    pallas_call x1, Pallas kernels, prepare(): pl.pallas_call(kernel, out_shape=jax.ShapeDtypeStruct((inner, wide_tile),...  3.82 us
  transfers between devices with their start and end apart: 17, of which 11 were waited for; matrix products, arithmetic and copies ran while one was open for 0% of the time, Pallas kernels for 9%

profile of v1, /device:TPU:0, one launch (start us, length us, event | category | flops | bytes accessed | tf_op | source)
XLA Modules:
  0.0 143.9 jit_solution(4414599839297614030)
XLA Ops:
  0.0 9.4 %shard_map.73 = (f32[32,4096]{1,0:T(8,128)S(1)}, bf16[32,4096]{1,0:T(8,128)(2,1)S(1)}) custom-call(s32[1]{0:T(128)} %bitcast.2.mask_ref, bf16[64,2048]{1,0:T(8,128)(2,1)} %query_hbm.2, bf16[2048,4096]{1,0:T(8,128)(2,1)} %basis_hbm.2), custom_call_target="tpu_custom_call" | custom-call | flops 1073741824 | bytes 16777216 | tf_op jit(solution)/shard_map/pallas_call | solution.py:67
  9.4 0.6 collective-permute-start
  10.0 1.2 collective-permute-done
  11.2 2.9 %collective-permute-start.1 = (bf16[32,2048]{1,0:T(8,128)(2,1)S(1)}, bf16[32,2048]{1,0:T(8,128)(2,1)S(1)}, u32[]{:S(2)}, u32[]{:S(2)}) collective-permute-start(bf16[32,2048]{1,0:T(8,128)(2,1)S(1)} %get-tuple-element.21), channel_id=1, source_target_pairs={{0,8},{4,12},{8,0},{12,4},{16,24},{20,28},{24,16},{28,20},{1,9},{5... | collective-permute-start | bytes 393224 | tf_op jit(solution)/shard_map/ppermute | solution.py:245
  14.2 1.5 %collective-permute-start.3 = (bf16[32,2048]{1,0:T(8,128)(2,1)S(1)}, bf16[32,2048]{1,0:T(8,128)(2,1)S(1)}, u32[]{:S(2)}, u32[]{:S(2)}) collective-permute-start(bf16[32,2048]{1,0:T(8,128)(2,1)S(1)} %get-tuple-element.22), channel_id=1, source_target_pairs={{0,16},{4,20},{8,24},{12,28},{16,0},{20,4},{24,8},{28,12},{1,17},{... | collective-permute-start | bytes 393224 | tf_op jit(solution)/shard_map/ppermute | solution.py:245
  15.7 2.3 %collective-permute-done.1 = bf16[32,2048]{1,0:T(8,128)(2,1)S(1)} collective-permute-done((bf16[32,2048]{1,0:T(8,128)(2,1)S(1)}, bf16[32,2048]{1,0:T(8,128)(2,1)S(1)}, u32[]{:S(2)}, u32[]{:S(2)}) %collective-permute-start.1) | collective-permute-done | bytes 131104 | tf_op jit(solution)/shard_map/ppermute | solution.py:245
  18.0 1.5 %collective-permute-done.3 = bf16[32,2048]{1,0:T(8,128)(2,1)S(1)} collective-permute-done((bf16[32,2048]{1,0:T(8,128)(2,1)S(1)}, bf16[32,2048]{1,0:T(8,128)(2,1)S(1)}, u32[]{:S(2)}, u32[]{:S(2)}) %collective-permute-start.3) | collective-permute-done | bytes 131104 | tf_op jit(solution)/shard_map/ppermute | solution.py:245
  19.5 1.6 %collective-permute-start.2 = (bf16[32,2048]{1,0:T(8,128)(2,1)S(1)}, bf16[32,2048]{1,0:T(8,128)(2,1)S(1)}, u32[]{:S(2)}, u32[]{:S(2)}) collective-permute-start(bf16[32,2048]{1,0:T(8,128)(2,1)S(1)} %get-tuple-element.19), channel_id=1, source_target_pairs={{0,16},{4,20},{8,24},{12,28},{16,0},{20,4},{24,8},{28,12},{1,17},{... | collective-permute-start | bytes 393224 | tf_op jit(solution)/shard_map/ppermute | solution.py:245
  21.1 0.5 collective-permute-start.4
  21.6 9.7 %shard_map.74 = (f32[16,2048]{1,0:T(8,128)S(1)}, bf16[16,2048]{1,0:T(8,128)(2,1)S(1)}, bf16[16,2048]{1,0:T(8,128)(2,1)S(1)}, bf16[16,2048]{1,0:T(8,128)(2,1)S(1)}) custom-call(s32[1]{0:T(128)} %bitcast.1.mask_ref, bf16[64,4096]{1,0:T(8,128)(2,1)} %query_hbm.3, bf16[4096,2048]{1,0:T(8,128)(2,1)} %basis_hbm.3), custom_call_target="tpu_custom_call" | custom-call | flops 1073741824 | bytes 16777216 | tf_op jit(solution)/shard_map/pallas_call | solution.py:67
  31.3 1.6 %collective-permute-start.6 = (bf16[16,2048]{1,0:T(8,128)(2,1)S(1)}, bf16[16,2048]{1,0:T(8,128)(2,1)S(1)}, u32[]{:S(2)}, u32[]{:S(2)}) collective-permute-start(bf16[16,2048]{1,0:T(8,128)(2,1)S(1)} %get-tuple-element.14), channel_id=1, source_target_pairs={{0,1},{1,0},{2,3},{3,2},{4,5},{5,4},{6,7},{7,6},{8,9},{9,8},{10,11... | collective-permute-start | bytes 196616 | tf_op jit(solution)/shard_map/ppermute | solution.py:245
  32.9 2.6 %collective-permute-start.7 = (bf16[16,2048]{1,0:T(8,128)(2,1)S(1)}, bf16[16,2048]{1,0:T(8,128)(2,1)S(1)}, u32[]{:S(2)}, u32[]{:S(2)}) collective-permute-start(bf16[16,2048]{1,0:T(8,128)(2,1)S(1)} %get-tuple-element.15), channel_id=1, source_target_pairs={{0,2},{1,3},{2,0},{3,1},{4,6},{5,7},{6,4},{7,5},{8,10},{9,11},{10,... | collective-permute-start | bytes 196616 | tf_op jit(solution)/shard_map/ppermute | solution.py:245
  35.5 0.0 copy-start.1
  35.5 0.0 copy-start.2
  35.5 0.2 collective-permute-start.8
  35.7 3.8 %shard_map.75.refs_6_ = bf16[2048,1024]{1,0:T(8,128)(2,1)S(1)} custom-call(f32[2048,4096]{1,0:T(8,128)} %refs_7_.1), custom_call_target="tpu_custom_call" | custom-call | flops 2097152 | bytes 12582912 | tf_op jit(solution)/shard_map/pallas_call | solution.py:107
  39.6 0.0 copy-start
  39.6 1.9 %copy-done = bf16[2048,1024]{1,0:T(8,128)(2,1)} copy-done((bf16[2048,1024]{1,0:T(8,128)(2,1)}, bf16[2048,1024]{1,0:T(8,128)(2,1)S(1)}, u32[]{:S(2)}) %copy-start) | copy-done | bytes 4194328
  41.5 0.0 collective-permute-done.2
  41.5 0.0 collective-permute-done.4
  41.5 0.1 add_convert_fusion.1
  41.6 0.1 collective-permute-start.5
  41.7 0.0 collective-permute-done.6
  41.7 0.0 collective-permute-done.7
  41.7 0.0 collective-permute-done.8
  41.8 3.7 %collective-permute-start.11 = (bf16[16,2048]{1,0:T(8,128)(2,1)S(1)}, bf16[16,2048]{1,0:T(8,128)(2,1)S(1)}, u32[]{:S(2)}, u32[]{:S(2)}) collective-permute-start(bf16[16,2048]{1,0:T(8,128)(2,1)S(1)} %add_convert_fusion.2.refs_0_), channel_id=1, source_target_pairs={{0,3},{1,2},{2,1},{3,0},{4,7},{5,6},{6,5},{7,4},{8,11},{9,10},{10,... | collective-permute-start | bytes 196616 | tf_op jit(solution)/shard_map/ppermute | solution.py:245
  45.4 0.0 collective-permute-start.10
  45.5 0.8 collective-permute-start.9
  46.2 0.1 pad_add_fusion.marks_ref
  46.3 2.3 %collective-permute-done.11.refs_3_ = bf16[16,2048]{1,0:T(8,128)(2,1)S(1)} collective-permute-done((bf16[16,2048]{1,0:T(8,128)(2,1)S(1)}, bf16[16,2048]{1,0:T(8,128)(2,1)S(1)}, u32[]{:S(2)}, u32[]{:S(2)}) %collective-permute-start.11) | collective-permute-done | bytes 65568 | tf_op jit(solution)/shard_map/ppermute | solution.py:245
  48.6 2.5 %collective-permute-done.10.refs_2_ = bf16[16,2048]{1,0:T(8,128)(2,1)S(1)} collective-permute-done((bf16[16,2048]{1,0:T(8,128)(2,1)S(1)}, bf16[16,2048]{1,0:T(8,128)(2,1)S(1)}, u32[]{:S(2)}, u32[]{:S(2)}) %collective-permute-start.10) | collective-permute-done | bytes 65568 | tf_op jit(solution)/shard_map/ppermute | solution.py:245
  51.1 0.1 collective-permute-done.9.refs_1_
  51.2 0.0 collective-permute-done.5.other_ref
  51.2 0.0 copy-done.1
  51.2 0.0 copy-done.2
  51.3 74.1 %shard_map.76 = f32[64,64]{1,0:T(8,128)S(1)} custom-call(s32[2]{0:T(128)S(1)} %pad_add_fusion.marks_ref, bf16[32,4096]{1,0:T(8,128)(2,1)S(1)} %pad_maximum_fusion.own_ref, bf16[32,4096]{1,0:T(8,128)(2,1)S(1)} %collective-permute-done.5.other_ref, bf16[16,2048]{1,0:T(8,128)(2,1)S(1)} %add_convert_fusion.2.refs_0_, ...), custom_call_target="tpu_custom_call" | custom-call | tf_op jit(solution)/shard_map/pallas_call | solution.py:212
  125.4 0.1 collective-permute-start.12
  125.5 1.2 collective-permute-done.12
  126.7 1.5 %collective-permute-start.13 = (f32[64,64]{1,0:T(8,128)S(1)}, f32[64,64]{1,0:T(8,128)S(1)}, u32[]{:S(2)}, u32[]{:S(2)}) collective-permute-start(f32[64,64]{1,0:T(8,128)S(1)} %add.47), channel_id=1, source_target_pairs={{0,8},{4,12},{8,0},{12,4},{16,24},{20,28},{24,16},{28,20},{1,9},{5... | collective-permute-start | bytes 49160 | tf_op jit(solution)/shard_map/ppermute | solution.py:245
  128.2 2.4 %collective-permute-done.13 = f32[64,64]{1,0:T(8,128)S(1)} collective-permute-done((f32[64,64]{1,0:T(8,128)S(1)}, f32[64,64]{1,0:T(8,128)S(1)}, u32[]{:S(2)}, u32[]{:S(2)}) %collective-permute-start.13) | collective-permute-done | bytes 16416 | tf_op jit(solution)/shard_map/ppermute | solution.py:245
  130.6 0.4 collective-permute-start.14
  131.0 3.5 %collective-permute-done.14 = f32[64,64]{1,0:T(8,128)S(1)} collective-permute-done((f32[64,64]{1,0:T(8,128)S(1)}, f32[64,64]{1,0:T(8,128)S(1)}, u32[]{:S(2)}, u32[]{:S(2)}) %collective-permute-start.14) | collective-permute-done | bytes 16416 | tf_op jit(solution)/shard_map/ppermute | solution.py:245
  134.5 1.5 %collective-permute-start.15 = (f32[64,64]{1,0:T(8,128)S(1)}, f32[64,64]{1,0:T(8,128)S(1)}, u32[]{:S(2)}, u32[]{:S(2)}) collective-permute-start(f32[64,64]{1,0:T(8,128)S(1)} %add.49), channel_id=1, source_target_pairs={{0,1},{1,0},{2,3},{3,2},{4,5},{5,4},{6,7},{7,6},{8,9},{9,8},{10,11... | collective-permute-start | bytes 49160 | tf_op jit(solution)/shard_map/ppermute | solution.py:245
  136.0 2.4 %collective-permute-done.15 = f32[64,64]{1,0:T(8,128)S(1)} collective-permute-done((f32[64,64]{1,0:T(8,128)S(1)}, f32[64,64]{1,0:T(8,128)S(1)}, u32[]{:S(2)}, u32[]{:S(2)}) %collective-permute-start.15) | collective-permute-done | bytes 16416 | tf_op jit(solution)/shard_map/ppermute | solution.py:245
  138.4 1.5 %collective-permute-start.16 = (f32[64,64]{1,0:T(8,128)S(1)}, f32[64,64]{1,0:T(8,128)S(1)}, u32[]{:S(2)}, u32[]{:S(2)}) collective-permute-start(f32[64,64]{1,0:T(8,128)S(1)} %add.50), channel_id=1, source_target_pairs={{0,2},{1,3},{2,0},{3,1},{4,6},{5,7},{6,4},{7,5},{8,10},{9,11},{10,... | collective-permute-start | bytes 49160 | tf_op jit(solution)/shard_map/ppermute | solution.py:245
  140.0 3.3 %collective-permute-done.16 = f32[64,64]{1,0:T(8,128)S(1)} collective-permute-done((f32[64,64]{1,0:T(8,128)S(1)}, f32[64,64]{1,0:T(8,128)S(1)}, u32[]{:S(2)}, u32[]{:S(2)}) %collective-permute-start.16) | collective-permute-done | bytes 16416 | tf_op jit(solution)/shard_map/ppermute | solution.py:245
  143.2 0.6 add_multiply_fusion
  (9 shorter events, 0.2 us)
Async XLA Ops:
  9.4 1.7 %collective-permute-start = (bf16[32,4096]{1,0:T(8,128)(2,1)S(1)}, bf16[32,4096]{1,0:T(8,128)(2,1)S(1)}, u32[]{:S(2)}, u32[]{:S(2)}) collective-permute-start(bf16[32,4096]{1,0:T(8,128)(2,1)S(1)} %get-tuple-element.12), channel_id=1, source_target_pairs={{0,4},{4,0},{8,12},{12,8},{16,20},{20,16},{24,28},{28,24},{1,5},{5... | collective-permute-start | bytes 786440 | tf_op jit(solution)/shard_map/ppermute | solution.py:245
  11.2 6.7 %collective-permute-start.1 = (bf16[32,2048]{1,0:T(8,128)(2,1)S(1)}, bf16[32,2048]{1,0:T(8,128)(2,1)S(1)}, u32[]{:S(2)}, u32[]{:S(2)}) collective-permute-start(bf16[32,2048]{1,0:T(8,128)(2,1)S(1)} %get-tuple-element.21), channel_id=1, source_target_pairs={{0,8},{4,12},{8,0},{12,4},{16,24},{20,28},{24,16},{28,20},{1,9},{5... | collective-permute-start | bytes 393224 | tf_op jit(solution)/shard_map/ppermute | solution.py:245
  14.2 5.3 %collective-permute-start.3 = (bf16[32,2048]{1,0:T(8,128)(2,1)S(1)}, bf16[32,2048]{1,0:T(8,128)(2,1)S(1)}, u32[]{:S(2)}, u32[]{:S(2)}) collective-permute-start(bf16[32,2048]{1,0:T(8,128)(2,1)S(1)} %get-tuple-element.22), channel_id=1, source_target_pairs={{0,16},{4,20},{8,24},{12,28},{16,0},{20,4},{24,8},{28,12},{1,17},{... | collective-permute-start | bytes 393224 | tf_op jit(solution)/shard_map/ppermute | solution.py:245
  19.5 22.1 %collective-permute-start.2 = (bf16[32,2048]{1,0:T(8,128)(2,1)S(1)}, bf16[32,2048]{1,0:T(8,128)(2,1)S(1)}, u32[]{:S(2)}, u32[]{:S(2)}) collective-permute-start(bf16[32,2048]{1,0:T(8,128)(2,1)S(1)} %get-tuple-element.19), channel_id=1, source_target_pairs={{0,16},{4,20},{8,24},{12,28},{16,0},{20,4},{24,8},{28,12},{1,17},{... | collective-permute-start | bytes 393224 | tf_op jit(solution)/shard_map/ppermute | solution.py:245
  21.1 20.5 %collective-permute-start.4 = (bf16[32,2048]{1,0:T(8,128)(2,1)S(1)}, bf16[32,2048]{1,0:T(8,128)(2,1)S(1)}, u32[]{:S(2)}, u32[]{:S(2)}) collective-permute-start(bf16[32,2048]{1,0:T(8,128)(2,1)S(1)} %get-tuple-element.20), channel_id=1, source_target_pairs={{0,8},{4,12},{8,0},{12,4},{16,24},{20,28},{24,16},{28,20},{1,9},{5... | collective-permute-start | bytes 393224 | tf_op jit(solution)/shard_map/ppermute | solution.py:245
  31.3 10.4 %collective-permute-start.6 = (bf16[16,2048]{1,0:T(8,128)(2,1)S(1)}, bf16[16,2048]{1,0:T(8,128)(2,1)S(1)}, u32[]{:S(2)}, u32[]{:S(2)}) collective-permute-start(bf16[16,2048]{1,0:T(8,128)(2,1)S(1)} %get-tuple-element.14), channel_id=1, source_target_pairs={{0,1},{1,0},{2,3},{3,2},{4,5},{5,4},{6,7},{7,6},{8,9},{9,8},{10,11... | collective-permute-start | bytes 196616 | tf_op jit(solution)/shard_map/ppermute | solution.py:245
  32.9 8.8 %collective-permute-start.7 = (bf16[16,2048]{1,0:T(8,128)(2,1)S(1)}, bf16[16,2048]{1,0:T(8,128)(2,1)S(1)}, u32[]{:S(2)}, u32[]{:S(2)}) collective-permute-start(bf16[16,2048]{1,0:T(8,128)(2,1)S(1)} %get-tuple-element.15), channel_id=1, source_target_pairs={{0,2},{1,3},{2,0},{3,1},{4,6},{5,7},{6,4},{7,5},{8,10},{9,11},{10,... | collective-permute-start | bytes 196616 | tf_op jit(solution)/shard_map/ppermute | solution.py:245
  35.5 15.7 %copy-start.1 = (bf16[64,4096]{1,0:T(8,128)(2,1)S(1)}, bf16[64,4096]{1,0:T(8,128)(2,1)}, u32[]{:S(2)}) copy-start(bf16[64,4096]{1,0:T(8,128)(2,1)} %refs_4_.1) | copy-start | bytes 1572868
  35.5 15.7 %copy-start.2 = (bf16[64,2048]{1,0:T(8,128)(2,1)S(1)}, bf16[64,2048]{1,0:T(8,128)(2,1)}, u32[]{:S(2)}) copy-start(bf16[64,2048]{1,0:T(8,128)(2,1)} %refs_5_.1) | copy-start | bytes 786436
  35.5 6.2 %collective-permute-start.8 = (bf16[16,2048]{1,0:T(8,128)(2,1)S(1)}, bf16[16,2048]{1,0:T(8,128)(2,1)S(1)}, u32[]{:S(2)}, u32[]{:S(2)}) collective-permute-start(bf16[16,2048]{1,0:T(8,128)(2,1)S(1)} %get-tuple-element.16), channel_id=1, source_target_pairs={{0,3},{1,2},{2,1},{3,0},{4,7},{5,6},{6,5},{7,4},{8,11},{9,10},{10,... | collective-permute-start | bytes 196616 | tf_op jit(solution)/shard_map/ppermute | solution.py:245
  39.6 1.9 %copy-start = (bf16[2048,1024]{1,0:T(8,128)(2,1)}, bf16[2048,1024]{1,0:T(8,128)(2,1)S(1)}, u32[]{:S(2)}) copy-start(bf16[2048,1024]{1,0:T(8,128)(2,1)S(1)} %shard_map.75.refs_6_) | copy-start | bytes 12582916
  41.6 9.6 %collective-permute-start.5 = (bf16[32,4096]{1,0:T(8,128)(2,1)S(1)}, bf16[32,4096]{1,0:T(8,128)(2,1)S(1)}, u32[]{:S(2)}, u32[]{:S(2)}) collective-permute-start(bf16[32,4096]{1,0:T(8,128)(2,1)S(1)} %pad_maximum_fusion.own_ref), channel_id=1, source_target_pairs={{0,4},{4,0},{8,12},{12,8},{16,20},{20,16},{24,28},{28,24},{1,5},{5... | collective-permute-start | bytes 786440 | tf_op jit(solution)/shard_map/ppermute | solution.py:245
  41.8 6.8 %collective-permute-start.11 = (bf16[16,2048]{1,0:T(8,128)(2,1)S(1)}, bf16[16,2048]{1,0:T(8,128)(2,1)S(1)}, u32[]{:S(2)}, u32[]{:S(2)}) collective-permute-start(bf16[16,2048]{1,0:T(8,128)(2,1)S(1)} %add_convert_fusion.2.refs_0_), channel_id=1, source_target_pairs={{0,3},{1,2},{2,1},{3,0},{4,7},{5,6},{6,5},{7,4},{8,11},{9,10},{10,... | collective-permute-start | bytes 196616 | tf_op jit(solution)/shard_map/ppermute | solution.py:245
  45.4 5.6 %collective-permute-start.10 = (bf16[16,2048]{1,0:T(8,128)(2,1)S(1)}, bf16[16,2048]{1,0:T(8,128)(2,1)S(1)}, u32[]{:S(2)}, u32[]{:S(2)}) collective-permute-start(bf16[16,2048]{1,0:T(8,128)(2,1)S(1)} %add_convert_fusion.2.refs_0_), channel_id=1, source_target_pairs={{0,2},{1,3},{2,0},{3,1},{4,6},{5,7},{6,4},{7,5},{8,10},{9,11},{10,... | collective-permute-start | bytes 196616 | tf_op jit(solution)/shard_map/ppermute | solution.py:245
  45.5 5.8 %collective-permute-start.9 = (bf16[16,2048]{1,0:T(8,128)(2,1)S(1)}, bf16[16,2048]{1,0:T(8,128)(2,1)S(1)}, u32[]{:S(2)}, u32[]{:S(2)}) collective-permute-start(bf16[16,2048]{1,0:T(8,128)(2,1)S(1)} %add_convert_fusion.2.refs_0_), channel_id=1, source_target_pairs={{0,1},{1,0},{2,3},{3,2},{4,5},{5,4},{6,7},{7,6},{8,9},{9,8},{10,11... | collective-permute-start | bytes 196616 | tf_op jit(solution)/shard_map/ppermute | solution.py:245
  125.4 1.3 collective-permute-start.12
  126.7 3.9 %collective-permute-start.13 = (f32[64,64]{1,0:T(8,128)S(1)}, f32[64,64]{1,0:T(8,128)S(1)}, u32[]{:S(2)}, u32[]{:S(2)}) collective-permute-start(f32[64,64]{1,0:T(8,128)S(1)} %add.47), channel_id=1, source_target_pairs={{0,8},{4,12},{8,0},{12,4},{16,24},{20,28},{24,16},{28,20},{1,9},{5... | collective-permute-start | bytes 49160 | tf_op jit(solution)/shard_map/ppermute | solution.py:245
  130.6 3.9 %collective-permute-start.14 = (f32[64,64]{1,0:T(8,128)S(1)}, f32[64,64]{1,0:T(8,128)S(1)}, u32[]{:S(2)}, u32[]{:S(2)}) collective-permute-start(f32[64,64]{1,0:T(8,128)S(1)} %add.48), channel_id=1, source_target_pairs={{0,16},{4,20},{8,24},{12,28},{16,0},{20,4},{24,8},{28,12},{1,17},{... | collective-permute-start | bytes 49160 | tf_op jit(solution)/shard_map/ppermute | solution.py:245
  134.5 3.9 %collective-permute-start.15 = (f32[64,64]{1,0:T(8,128)S(1)}, f32[64,64]{1,0:T(8,128)S(1)}, u32[]{:S(2)}, u32[]{:S(2)}) collective-permute-start(f32[64,64]{1,0:T(8,128)S(1)} %add.49), channel_id=1, source_target_pairs={{0,1},{1,0},{2,3},{3,2},{4,5},{5,4},{6,7},{7,6},{8,9},{9,8},{10,11... | collective-permute-start | bytes 49160 | tf_op jit(solution)/shard_map/ppermute | solution.py:245
  138.4 4.8 %collective-permute-start.16 = (f32[64,64]{1,0:T(8,128)S(1)}, f32[64,64]{1,0:T(8,128)S(1)}, u32[]{:S(2)}, u32[]{:S(2)}) collective-permute-start(f32[64,64]{1,0:T(8,128)S(1)} %add.50), channel_id=1, source_target_pairs={{0,2},{1,3},{2,0},{3,1},{4,6},{5,7},{6,4},{7,5},{8,10},{9,11},{10,... | collective-permute-start | bytes 49160 | tf_op jit(solution)/shard_map/ppermute | solution.py:245
